TPU v7x, 32 devices: a whole 2x2x4 slice. The times are simulated.
32 devices in a mesh: row: 4 (over y, core), col: 8 (over z, x).
Axes of the slice: x: 2, y: 2, z: 4, core: 2. Of those that a mesh axis runs over, the one named last changes fastest.
Arguments:
- transfer: bfloat16 [2048, 2, 512, 256], P(('row', 'col')), may hold values from -0.65625 to 0.65625
- target: bfloat16 [2048, 2, 32, 512], P(('row', 'col')), may hold values from -6 to 6
- zone_mask: int32 [32, 512], replicated, may hold values 0 or 1
- dark_weight: float32 [32], replicated, may hold values from 1 to 4
- reg_weight: float32 [2048], P(('row', 'col')), may hold values from 0.05 to 2
- momentum: float32 [1], replicated, may hold values from 0.2 to 0.8
Outputs:
- filters: float32 [32, 256, 1024], P(None, ('row', 'col'))
- residual: float32 [32, 256, 1024], P(None, ('row', 'col'))
All inputs are finite; a program needn't handle non-finite values.
Results may differ from a plain program's by a relative error of at most 0.0059.
Values may be sent and summed in bfloat16 or wider, within the bound.
No kernel may reach another device: no remote copies, remote signals or barrier semaphores. Data moves between devices by JAX's collectives and lax.ppermute only.
A program may use at most 128 MiB of HBM per device.

v0:
```python
import math
import jax
import jax.numpy as jnp
from jax import lax
from jax.sharding import PartitionSpec as P

K = 1024
F = 2048
ITERS = 2


def build_table(taps, bins):
    tap_index = jnp.arange(taps, dtype=jnp.int32)[:, None]
    bin_index = jnp.arange(bins, dtype=jnp.int32)[None, :]
    phase = (tap_index * bin_index % bins).astype(jnp.float32) * (2.0 * math.pi / bins)
    return jnp.stack([jnp.cos(phase), -jnp.sin(phase)], axis=1) / math.sqrt(bins)


def body(transfer, target, zone_mask, dark_weight, reg_weight, momentum):
    dft_table = build_table(K, F)
    mic_gains = jnp.where(zone_mask == 1, jnp.float32(1.0), dark_weight[:, None])
    weight_real = transfer[:, 0]
    weight_imag = transfer[:, 1]
    reg_term = reg_weight[:, None, None]

    def to_taps(spectrum):
        regrouped = lax.all_to_all(
            spectrum, ("row", "col"), split_axis=3, concat_axis=0, tiled=True
        )
        return jnp.einsum("fctl,kcf->tlk", regrouped, dft_table, precision=lax.Precision.HIGHEST)

    def back_project(err_real, err_imag):
        back_real = jnp.einsum(
            "fml,ftm->ftl", weight_real, err_real, preferred_element_type=jnp.float32
        )
        back_real = back_real + jnp.einsum(
            "fml,ftm->ftl", weight_imag, err_imag, preferred_element_type=jnp.float32
        )
        back_imag = jnp.einsum(
            "fml,ftm->ftl", weight_real, err_imag, preferred_element_type=jnp.float32
        )
        back_imag = back_imag - jnp.einsum(
            "fml,ftm->ftl", weight_imag, err_real, preferred_element_type=jnp.float32
        )
        return (back_real, back_imag)

    rhs_error = jnp.where(zone_mask[None, None] == 1, target, jnp.zeros_like(target))
    rhs_real, rhs_imag = back_project(rhs_error[:, 0], rhs_error[:, 1])
    rhs = to_taps(jnp.stack([rhs_real, rhs_imag], axis=1))
    filters = jnp.zeros_like(rhs)
    residual = rhs
    direction = rhs
    for iteration in range(ITERS):
        along_term = jnp.sum(residual * direction)
        to_spectrum = jnp.einsum(
            "tlk,kcf->fctl", direction, dft_table, precision=lax.Precision.HIGHEST
        ).astype(jnp.bfloat16)
        to_regrouped = lax.all_to_all(
            to_spectrum, ("row", "col"), split_axis=0, concat_axis=3, tiled=True
        )
        spec_real = to_regrouped[:, 0]
        spec_imag = to_regrouped[:, 1]
        press_real = jnp.einsum(
            "fml,ftl->ftm", weight_real, spec_real, preferred_element_type=jnp.float32
        )
        press_real = press_real - jnp.einsum(
            "fml,ftl->ftm", weight_imag, spec_imag, preferred_element_type=jnp.float32
        )
        press_imag = jnp.einsum(
            "fml,ftl->ftm", weight_real, spec_imag, preferred_element_type=jnp.float32
        )
        press_imag = press_imag + jnp.einsum(
            "fml,ftl->ftm", weight_imag, spec_real, preferred_element_type=jnp.float32
        )
        weighted_real = mic_gains * press_real
        weighted_imag = mic_gains * press_imag
        operator_back_real, operator_back_imag = back_project(
            weighted_real.astype(jnp.bfloat16), weighted_imag.astype(jnp.bfloat16)
        )
        wide_real = spec_real.astype(jnp.float32)
        wide_imag = spec_imag.astype(jnp.float32)
        totals = None
        combined = jnp.stack(
            [operator_back_real + reg_term * wide_real, operator_back_imag + reg_term * wide_imag],
            axis=1,
        )
        image_taps, totals = (to_taps(combined), totals)
        along_sum, bend_sum = lax.psum(
            (along_term, jnp.sum(direction * image_taps)), ("row", "col")
        )
        step_size = along_sum / bend_sum
        filters = filters + step_size * direction
        residual = residual - step_size * image_taps
        if iteration + 1 < ITERS:
            direction = residual + momentum[iteration] * direction
    return (filters, residual)


def solution(mesh):
    in_specs = (
        P(("row", "col"), None, None, None),
        P(("row", "col"), None, None, None),
        P(),
        P(),
        P(("row", "col")),
        P(),
    )
    out_specs = (P(None, ("row", "col"), None), P(None, ("row", "col"), None))
    return jax.shard_map(body, mesh=mesh, in_specs=in_specs, out_specs=out_specs, check_vma=False)
```

profile of v0, /device:TPU:0, one launch (start us, length us, event | category | flops | bytes accessed | tf_op | source)
XLA Modules:
  0.0 1125.6 jit_solution(2938262932582563198)
XLA Ops:
  35.3 9.2 copy.60
  44.5 9.8 reshape.84
  62.3 34.6 %sine_negate_fusion = (f32[1024,1,2048]{2,0,1:T(8,128)}, f32[1024,1,2048]{2,0,1:T(8,128)}) fusion(), kind=kLoop, calls=%fused_computation.57 | loop fusion | flops 31457280 | bytes 16777216 | tf_op jit(solution)/shard_map/neg | solution.py:16
  96.8 60.6 %all-to-all-done = f32[32,1,32768]{2,1,0:T(1,128)} async-done(((f32[32,1,32768]{2,1,0:T(1,128)}), f32[32,1,32768]{2,1,0:T(1,128)}, u32[]{:S(2)}, u32[]{:S(2)}) %all-to-all-start) | async-done | bytes 4194336 | tf_op jit(solution)/shard_map/all_to_all | solution.py:27
  158.0 13.8 %reduce = f32[32,32768]{1,0:T(8,128)} reduce(f32[32,1,32768]{2,1,0:T(1,128)} %all-to-all-done, f32[]{:T(128)} %broadcast.90), dimensions={1}, to_apply=%all_to_all.65.reduce_sub_computation | reduce | bytes 8388612 | tf_op jit(solution)/shard_map/all_to_all | solution.py:27
  179.1 11.4 %copy.62 = f32[32,64,2,32,8]{1,0,4,2,3:T(8,128)} copy(f32[32,64,2,32,8]{1,3,2,4,0:T(8,128)} %bitcast.207) | data formatting | bytes 8388608 | tf_op jit(solution)/shard_map/all_to_all | solution.py:27
  198.4 18.7 %fusion.81 = f32[32,8,1024]{2,1,0:T(8,128)S(1)} fusion(f32[2048,2,32,8]{0,3,1,2:T(8,128)} %all_to_all.68, f32[1024,1,2048]{2,0,1:T(8,128)} %get-tuple-element.20, f32[1024,1,2048]{2,0,1:T(8,128)} %get-tuple-element.21), kind=kOutput, calls=%fused_computation.90 | convolution fusion | flops 12893290496 | bytes 22020096 | tf_op jit(solution)/shard_map/fctl,kcf->tlk/dot_general | solution.py:30
  218.0 19.9 %fusion.66 = bf16[2048,2,32,8]{0,2,3,1:T(8,128)(2,1)S(1)} fusion(f32[32,8,1024]{2,1,0:T(8,128)S(1)} %fusion.81, f32[1024,1,2048]{2,0,1:T(8,128)} %get-tuple-element.20, f32[1024,1,2048]{2,0,1:T(8,128)} %get-tuple-element.21), kind=kOutput, calls=%fused_computation.73 | convolution fusion | flops 12894339072 | bytes 19922944 | tf_op jit(solution)/shard_map/tlk,kcf->fctl/dot_general | solution.py:55
  246.5 12.2 %reshape.86 = bf16[32,2,16384]{2,1,0:T(2,128)(2,1)S(1)} reshape(bf16[2048,2,8,32]{3,2,1,0:T(8,128)(2,1)} %bitcast.200) | data formatting | bytes 4194304
  258.8 52.7 %all_to_all.90 = bf16[32,2,16384]{2,1,0:T(2,128)(2,1)} all-to-all(bf16[32,2,16384]{2,1,0:T(2,128)(2,1)S(1)} %reshape.86), channel_id=1, replica_groups=mesh['row'=4,'col'=8] {'row','col'}, dimensions={0} | all-to-all | bytes 4194304 | tf_op jit(solution)/shard_map/all_to_all | solution.py:58
  311.5 11.7 %reshape.87 = bf16[2048,2,8,32]{3,2,1,0:T(8,128)(2,1)} reshape(bf16[32,2,16384]{2,1,0:T(2,128)(2,1)} %all_to_all.90) | data formatting | bytes 4194304
  323.2 12.1 %copy.65 = bf16[32,64,2,32,8]{1,4,0,3,2:T(8,128)(2,1)} copy(bf16[32,64,2,32,8]{3,4,2,1,0:T(8,128)(2,1)} %bitcast.201) | data formatting | bytes 4194304 | tf_op jit(solution)/shard_map/all_to_all | solution.py:58
  342.7 12.7 %fusion.12 = f32[64,32,512]{2,1,0:T(8,128)} fusion(bf16[64,1,32,256]{3,2,0,1:T(8,128)(2,1)S(1)} %copy.88, bf16[64,2,512,256]{3,2,1,0:T(8,128)(2,1)} %param.6), kind=kOutput, calls=%fused_computation.13 | convolution fusion | flops 536870912 | bytes 22020096 | tf_op jit(solution)/shard_map/fml,ftl->ftm/dot_general | solution.py:72
  355.4 12.7 %fusion.34 = f32[64,32,512]{2,1,0:T(8,128)} fusion(bf16[64,1,32,256]{3,2,0,1:T(8,128)(2,1)S(1)} %copy.88, bf16[64,2,512,256]{3,2,1,0:T(8,128)(2,1)} %param.6), kind=kOutput, calls=%fused_computation.35 | convolution fusion | flops 536870912 | bytes 22020096 | tf_op jit(solution)/shard_map/fml,ftl->ftm/dot_general | solution.py:63
  371.2 12.7 %fusion.30 = f32[64,32,512]{2,1,0:T(8,128)} fusion(bf16[64,1,32,256]{3,2,0,1:T(8,128)(2,1)S(1)} %copy.89, bf16[64,2,512,256]{3,2,1,0:T(8,128)(2,1)} %param.6), kind=kOutput, calls=%fused_computation.31 | convolution fusion | flops 536870912 | bytes 22020096 | tf_op jit(solution)/shard_map/fml,ftl->ftm/dot_general | solution.py:69
  383.9 12.7 %fusion.14 = f32[64,32,512]{2,1,0:T(8,128)} fusion(bf16[64,1,32,256]{3,2,0,1:T(8,128)(2,1)S(1)} %copy.89, bf16[64,2,512,256]{3,2,1,0:T(8,128)(2,1)} %param.6), kind=kOutput, calls=%fused_computation.15 | convolution fusion | flops 536870912 | bytes 22020096 | tf_op jit(solution)/shard_map/fml,ftl->ftm/dot_general | solution.py:66
  396.6 11.9 %fusion.10 = f32[64,32,256]{2,1,0:T(8,128)} fusion(f32[64,32,512]{2,1,0:T(8,128)} %fusion.30, f32[64,32,512]{2,1,0:T(8,128)} %fusion.12, f32[32,512]{1,0:T(8,128)S(1)} %get-tuple-element.10, bf16[64,2,512,256]{3,2,1,0:T(8,128)(2,1)} %param.6), kind=kOutput, calls=%fused_computation.11 | convolution fusion | flops 540016640 | bytes 27328512 | tf_op jit(solution)/shard_map/fml,ftm->ftl/dot_general | solution.py:36
  408.5 11.9 %fusion.8 = f32[64,32,256]{2,1,0:T(8,128)} fusion(f32[64,32,512]{2,1,0:T(8,128)} %fusion.34, f32[64,32,512]{2,1,0:T(8,128)} %fusion.14, f32[32,512]{1,0:T(8,128)S(1)} %get-tuple-element.10, bf16[64,2,512,256]{3,2,1,0:T(8,128)(2,1)} %param.6), kind=kOutput, calls=%fused_computation.9 | convolution fusion | flops 540016640 | bytes 27328512 | tf_op jit(solution)/shard_map/fml,ftm->ftl/dot_general | solution.py:42
  420.4 12.8 %add_bitcast_fusion.3 = f32[64,1,32,256]{3,2,0,1:T(8,128)} fusion(f32[64,32,256]{2,1,0:T(8,128)} %fusion.10, f32[64,32,512]{2,1,0:T(8,128)} %fusion.34, f32[64,32,512]{2,1,0:T(8,128)} %fusion.14, f32[32,512]{1,0:T(8,128)S(1)} %get-tuple-element.10, bf16[64,1,32,256]{3,2,0,1:T(8,128)(2,1)S(1)} %copy.88, f32[64]{0:T(128)S(1)} %copy-done.9, ...), kind=kOutput, calls=%fused_computation.79 | convolution fusion | flops 542113792 | bytes 30474496 | tf_op jit(solution)/shard_map/fml,ftm->ftl/dot_general | solution.py:33
  433.3 13.1 %add_bitcast_fusion.2 = f32[64,1,32,256]{3,2,0,1:T(8,128)} fusion(f32[64,32,256]{2,1,0:T(8,128)} %fusion.8, f32[64,32,512]{2,1,0:T(8,128)} %fusion.30, f32[64,32,512]{2,1,0:T(8,128)} %fusion.12, f32[32,512]{1,0:T(8,128)S(1)} %get-tuple-element.10, bf16[64,1,32,256]{3,2,0,1:T(8,128)(2,1)S(1)} %copy.89, f32[64]{0:T(128)S(1)} %copy-done.9, ...), kind=kOutput, calls=%fused_computation.78 | convolution fusion | flops 542113792 | bytes 30474496 | tf_op jit(solution)/shard_map/fml,ftm->ftl/dot_general | solution.py:39
  450.3 9.2 copy.68
  459.5 9.8 reshape.88
  473.6 94.5 %all-to-all-done.2 = f32[32,1,32768]{2,1,0:T(1,128)} async-done(((f32[32,1,32768]{2,1,0:T(1,128)}), f32[32,1,32768]{2,1,0:T(1,128)}, u32[]{:S(2)}, u32[]{:S(2)}) %all-to-all-start.2) | async-done | bytes 4194336 | tf_op jit(solution)/shard_map/all_to_all | solution.py:27
  568.1 13.8 %reduce.1 = f32[32,32768]{1,0:T(8,128)} reduce(f32[32,1,32768]{2,1,0:T(1,128)} %all-to-all-done.2, f32[]{:T(128)} %broadcast.90), dimensions={1}, to_apply=%all_to_all.73.reduce_sub_computation | reduce | bytes 8388612 | tf_op jit(solution)/shard_map/all_to_all | solution.py:27
  589.2 11.4 %copy.70 = f32[32,64,2,32,8]{1,0,4,2,3:T(8,128)} copy(f32[32,64,2,32,8]{1,3,2,4,0:T(8,128)} %bitcast.208) | data formatting | bytes 8388608 | tf_op jit(solution)/shard_map/all_to_all | solution.py:27
  608.5 19.5 %multiply_reduce_fusion.2 = (f32[]{:T(128)}, f32[]{:T(128)}, f32[32,8,1024]{2,1,0:T(8,128)S(1)}) fusion(f32[32,8,1024]{2,1,0:T(8,128)S(1)} %copy-done.3, f32[2048,2,32,8]{0,3,1,2:T(8,128)} %all_to_all.76, f32[1024,1,2048]{2,0,1:T(8,128)} %get-tuple-element.20, f32[1024,1,2048]{2,0,1:T(8,128)} %get-tuple-element.21), kind=kOutput, calls=%fused_computation.111 | convolution fusion | flops 12894339072 | bytes 23068680 | tf_op jit(solution)/shard_map/fctl,kcf->tlk/dot_general | solution.py:30
  628.1 37.4 %all-reduce.1 = (f32[]{:T(128)}, f32[]{:T(128)}) all-reduce(f32[]{:T(128)} %get-tuple-element.5, f32[]{:T(128)} %get-tuple-element.4), channel_id=1, replica_groups=mesh['row'=4,'col'=8] {'row','col'}, use_global_device_ids=true, to_apply=%region_1.2 | all-reduce | flops 2 | bytes 16 | tf_op jit(solution)/shard_map/psum | solution.py:88
  667.1 21.2 %fusion.63 = bf16[2048,2,32,8]{0,2,3,1:T(8,128)(2,1)} fusion(f32[32,8,1024]{2,1,0:T(8,128)S(1)} %multiply_add_fusion.1, f32[1024,1,2048]{2,0,1:T(8,128)} %get-tuple-element.20, f32[1024,1,2048]{2,0,1:T(8,128)} %get-tuple-element.21), kind=kOutput, calls=%fused_computation.72 | convolution fusion | flops 12894339072 | bytes 19922944 | tf_op jit(solution)/shard_map/tlk,kcf->fctl/dot_general | solution.py:55
  688.3 10.0 copy.72
  698.3 12.2 %reshape.90 = bf16[32,2,16384]{2,1,0:T(2,128)(2,1)S(1)} reshape(bf16[2048,2,8,32]{3,2,1,0:T(8,128)(2,1)} %bitcast.202) | data formatting | bytes 4194304
  710.5 55.8 %all_to_all.91 = bf16[32,2,16384]{2,1,0:T(2,128)(2,1)} all-to-all(bf16[32,2,16384]{2,1,0:T(2,128)(2,1)S(1)} %reshape.90), channel_id=1, replica_groups=mesh['row'=4,'col'=8] {'row','col'}, dimensions={0} | all-to-all | bytes 4194304 | tf_op jit(solution)/shard_map/all_to_all | solution.py:58
  766.3 11.7 %reshape.91 = bf16[2048,2,8,32]{3,2,1,0:T(8,128)(2,1)} reshape(bf16[32,2,16384]{2,1,0:T(2,128)(2,1)} %all_to_all.91) | data formatting | bytes 4194304
  778.0 12.1 %copy.73 = bf16[32,64,2,32,8]{1,4,0,3,2:T(8,128)(2,1)} copy(bf16[32,64,2,32,8]{3,4,2,1,0:T(8,128)(2,1)} %bitcast.203) | data formatting | bytes 4194304 | tf_op jit(solution)/shard_map/all_to_all | solution.py:58
  797.5 12.7 %fusion.4 = f32[64,32,512]{2,1,0:T(8,128)} fusion(bf16[64,1,32,256]{3,2,0,1:T(8,128)(2,1)S(1)} %copy.90, bf16[64,2,512,256]{3,2,1,0:T(8,128)(2,1)} %param.6), kind=kOutput, calls=%fused_computation.5 | convolution fusion | flops 536870912 | bytes 22020096 | tf_op jit(solution)/shard_map/fml,ftl->ftm/dot_general | solution.py:72
  810.2 12.7 %fusion.26 = f32[64,32,512]{2,1,0:T(8,128)} fusion(bf16[64,1,32,256]{3,2,0,1:T(8,128)(2,1)S(1)} %copy.90, bf16[64,2,512,256]{3,2,1,0:T(8,128)(2,1)} %param.6), kind=kOutput, calls=%fused_computation.27 | convolution fusion | flops 536870912 | bytes 22020096 | tf_op jit(solution)/shard_map/fml,ftl->ftm/dot_general | solution.py:63
  825.8 12.7 %fusion.22 = f32[64,32,512]{2,1,0:T(8,128)} fusion(bf16[64,1,32,256]{3,2,0,1:T(8,128)(2,1)S(1)} %copy.91, bf16[64,2,512,256]{3,2,1,0:T(8,128)(2,1)} %param.6), kind=kOutput, calls=%fused_computation.23 | convolution fusion | flops 536870912 | bytes 22020096 | tf_op jit(solution)/shard_map/fml,ftl->ftm/dot_general | solution.py:69
  838.5 12.7 %fusion.6 = f32[64,32,512]{2,1,0:T(8,128)} fusion(bf16[64,1,32,256]{3,2,0,1:T(8,128)(2,1)S(1)} %copy.91, bf16[64,2,512,256]{3,2,1,0:T(8,128)(2,1)} %param.6), kind=kOutput, calls=%fused_computation.7 | convolution fusion | flops 536870912 | bytes 22020096 | tf_op jit(solution)/shard_map/fml,ftl->ftm/dot_general | solution.py:66
  851.2 11.9 %fusion.2 = f32[64,32,256]{2,1,0:T(8,128)} fusion(f32[64,32,512]{2,1,0:T(8,128)} %fusion.22, f32[64,32,512]{2,1,0:T(8,128)} %fusion.4, f32[32,512]{1,0:T(8,128)S(1)} %get-tuple-element.10, bf16[64,2,512,256]{3,2,1,0:T(8,128)(2,1)} %param.6), kind=kOutput, calls=%fused_computation.3 | convolution fusion | flops 540016640 | bytes 27328512 | tf_op jit(solution)/shard_map/fml,ftm->ftl/dot_general | solution.py:36
  863.1 11.9 %fusion = f32[64,32,256]{2,1,0:T(8,128)} fusion(f32[64,32,512]{2,1,0:T(8,128)} %fusion.26, f32[64,32,512]{2,1,0:T(8,128)} %fusion.6, f32[32,512]{1,0:T(8,128)S(1)} %get-tuple-element.10, bf16[64,2,512,256]{3,2,1,0:T(8,128)(2,1)} %param.6), kind=kOutput, calls=%fused_computation.1 | convolution fusion | flops 540016640 | bytes 27328512 | tf_op jit(solution)/shard_map/fml,ftm->ftl/dot_general | solution.py:42
  875.0 12.8 %add_bitcast_fusion.1 = f32[64,1,32,256]{3,2,0,1:T(8,128)} fusion(f32[64,32,256]{2,1,0:T(8,128)} %fusion.2, f32[64,32,512]{2,1,0:T(8,128)} %fusion.26, f32[64,32,512]{2,1,0:T(8,128)} %fusion.6, f32[32,512]{1,0:T(8,128)S(1)} %get-tuple-element.10, bf16[64,1,32,256]{3,2,0,1:T(8,128)(2,1)S(1)} %copy.90, f32[64]{0:T(128)S(1)} %copy-done.9, ...), kind=kOutput, calls=%fused_computation.77 | convolution fusion | flops 542113792 | bytes 30474496 | tf_op jit(solution)/shard_map/fml,ftm->ftl/dot_general | solution.py:33
  887.9 13.1 %add_bitcast_fusion = f32[64,1,32,256]{3,2,0,1:T(8,128)} fusion(f32[64,32,256]{2,1,0:T(8,128)} %fusion, f32[64,32,512]{2,1,0:T(8,128)} %fusion.22, f32[64,32,512]{2,1,0:T(8,128)} %fusion.4, f32[32,512]{1,0:T(8,128)S(1)} %get-tuple-element.10, bf16[64,1,32,256]{3,2,0,1:T(8,128)(2,1)S(1)} %copy.91, f32[64]{0:T(128)S(1)} %copy-done.9, ...), kind=kOutput, calls=%fused_computation.76 | convolution fusion | flops 542113792 | bytes 30474496 | tf_op jit(solution)/shard_map/fml,ftm->ftl/dot_general | solution.py:39
  905.0 9.2 copy.76
  914.2 9.8 reshape.92
  924.0 98.5 %all_to_all.92 = f32[32,1,32768]{2,1,0:T(1,128)} all-to-all(f32[32,1,32768]{2,1,0:T(1,128)} %reshape.92), channel_id=1, replica_groups=mesh['row'=4,'col'=8] {'row','col'}, dimensions={0} | all-to-all | bytes 8388608 | tf_op jit(solution)/shard_map/all_to_all | solution.py:27
  1022.5 13.8 %reduce.2 = f32[32,32768]{1,0:T(8,128)} reduce(f32[32,1,32768]{2,1,0:T(1,128)} %all_to_all.92, f32[]{:T(128)} %broadcast.90), dimensions={1}, to_apply=%all_to_all.81.reduce_sub_computation | reduce | bytes 8388612 | tf_op jit(solution)/shard_map/all_to_all | solution.py:27
  1043.6 11.4 %copy.78 = f32[32,64,2,32,8]{1,0,4,2,3:T(8,128)} copy(f32[32,64,2,32,8]{1,3,2,4,0:T(8,128)} %bitcast.209) | data formatting | bytes 8388608 | tf_op jit(solution)/shard_map/all_to_all | solution.py:27
  1063.1 19.6 %multiply_reduce_fusion = (f32[]{:T(128)}, f32[]{:T(128)}, f32[32,8,1024]{2,1,0:T(8,128)}) fusion(f32[32,8,1024]{2,1,0:T(8,128)S(1)} %copy-done.8, f32[32,8,1024]{2,1,0:T(8,128)S(1)} %copy-done.4, f32[32,8,1024]{2,1,0:T(8,128)S(1)} %copy-done.6, f32[]{:T(128)S(6)} %div.14, f32[2048,2,32,8]{0,3,1,2:T(8,128)} %all_to_all.84, ...), kind=kOutput, calls=%fused_computation.107 | convolution fusion | flops 12894863360 | bytes 25165836 | tf_op jit(solution)/shard_map/fctl,kcf->tlk/dot_general | solution.py:30
  1082.7 38.0 %all-reduce = (f32[]{:T(128)}, f32[]{:T(128)}) all-reduce(f32[]{:T(128)} %get-tuple-element.3, f32[]{:T(128)} %get-tuple-element.2), channel_id=1, replica_groups=mesh['row'=4,'col'=8] {'row','col'}, use_global_device_ids=true, to_apply=%region_5.6 | all-reduce | flops 2 | bytes 16 | tf_op jit(solution)/shard_map/psum | solution.py:88
  (47 shorter events, 134.1 us)
Async XLA Ops:
  54.3 103.1 %all-to-all-start = ((f32[32,1,32768]{2,1,0:T(1,128)}), f32[32,1,32768]{2,1,0:T(1,128)}, u32[]{:S(2)}, u32[]{:S(2)}) async-start(f32[32,1,32768]{2,1,0:T(1,128)} %reshape.84), calls=%async_computation | async-start | bytes 8388608 | tf_op jit(solution)/shard_map/all_to_all | solution.py:27
  217.1 1.0 copy-start.2
  408.5 11.9 %copy-start.9 = (f32[64]{0:T(128)S(1)}, f32[64]{0:T(128)}, u32[]{:S(2)}) copy-start(f32[64]{0:T(128)} %param.10) | copy-start | bytes 772
  433.2 13.1 %copy-start.1 = (f32[64,1,32,256]{3,2,0,1:T(8,128)S(1)}, f32[64,1,32,256]{3,2,0,1:T(8,128)}, u32[]{:S(2)}) copy-start(f32[64,1,32,256]{3,2,0,1:T(8,128)} %add_bitcast_fusion.3) | copy-start | bytes 6291460
  469.3 98.7 %all-to-all-start.2 = ((f32[32,1,32768]{2,1,0:T(1,128)}), f32[32,1,32768]{2,1,0:T(1,128)}, u32[]{:S(2)}, u32[]{:S(2)}) async-start(f32[32,1,32768]{2,1,0:T(1,128)} %reshape.88), calls=%async_computation.2 | async-start | bytes 8388608 | tf_op jit(solution)/shard_map/all_to_all | solution.py:27
  600.6 7.9 copy-start.3
  628.1 60.2 %copy-start.5 = (f32[32,8,1024]{2,1,0:T(8,128)}, f32[32,8,1024]{2,1,0:T(8,128)S(1)}, u32[]{:S(2)}) copy-start(f32[32,8,1024]{2,1,0:T(8,128)S(1)} %get-tuple-element.18) | copy-start | bytes 3145732
  667.1 21.2 %copy-start.7 = (f32[32,8,1024]{2,1,0:T(8,128)}, f32[32,8,1024]{2,1,0:T(8,128)S(1)}, u32[]{:S(2)}) copy-start(f32[32,8,1024]{2,1,0:T(8,128)S(1)} %multiply_add_fusion.1) | copy-start | bytes 3145732
  887.9 13.1 %copy-start = (f32[64,1,32,256]{3,2,0,1:T(8,128)S(1)}, f32[64,1,32,256]{3,2,0,1:T(8,128)}, u32[]{:S(2)}) copy-start(f32[64,1,32,256]{3,2,0,1:T(8,128)} %add_bitcast_fusion.1) | copy-start | bytes 6291460
  1055.1 8.0 copy-start.4
  1055.1 8.0 copy-start.6
  1055.1 8.0 copy-start.8
where the time goes:
time: 1140 us; the launch traced here: 1130 us
  matrix products  329 us (29%)
  blocking collectives  283 us (25%)
  local copies, waits for them, and re-layouts  250 us (22%)
  waiting for transfers between devices  155 us (14%)
  other arithmetic  93.1 us (8%)
  starting transfers between devices  11.5 us (1%)
    all_to_all x2, waiting for transfers between devices, to_taps(): lax.all_to_all(spectrum, ('row', 'col'), split_axis=3, concat_axis=0, til...  155 us
    unnamed x34, local copies, waits for them, and re-layouts  112 us
    all_to_all x2, blocking collectives, body(): lax.all_to_all(to_spectrum, ('row', 'col'), split_axis=0, concat_axis=3,...  109 us
    all_to_all x1, blocking collectives, to_taps(): lax.all_to_all(spectrum, ('row', 'col'), split_axis=3, concat_axis=0, til...  98.5 us
    psum x2, blocking collectives, body(): lax.psum((along_term, jnp.sum(direction * image_taps)), ('row', 'col'))  75.5 us
    all_to_all x7, local copies, waits for them, and re-layouts, to_taps(): lax.all_to_all(spectrum, ('row', 'col'), split_axis=3, concat_axis=0, til...  58.6 us
    dot_general x3, matrix products, to_taps(): jnp.einsum('fctl,kcf->tlk', regrouped, dft_table, precision=lax.Precision...  57.9 us
    all_to_all x3, other arithmetic, to_taps(): lax.all_to_all(spectrum, ('row', 'col'), split_axis=3, concat_axis=0, til...  41.3 us
  transfers between devices with their start and end apart: 2, of which 2 were waited for; matrix products, arithmetic and copies ran while one was open for 3% of the time, Pallas kernels for 0%

commit v1 on v0

--- a/solution.py
+++ b/solution.py
@@ -55,8 +55,14 @@
         to_spectrum = jnp.einsum(
             "tlk,kcf->fctl", direction, dft_table, precision=lax.Precision.HIGHEST
         ).astype(jnp.bfloat16)
-        to_regrouped = lax.all_to_all(
-            to_spectrum, ("row", "col"), split_axis=0, concat_axis=3, tiled=True
+        to_regrouped = jnp.concatenate(
+            lax.all_to_all(
+                jnp.stack(jnp.split(to_spectrum, lax.axis_size(("row", "col")), axis=0)),
+                ("row", "col"),
+                0,
+                0,
+            ),
+            axis=3,
         )
         spec_real = to_regrouped[:, 0]
         spec_imag = to_regrouped[:, 1]

time: 1140 us -> 1090 us (0.956)
  local copies, waits for them, and re-layouts: 250 us -> 203 us
    all_to_all x2 -> x0, local copies, waits for them, and re-layouts: 24.3 us -> none  [body(): lax.all_to_all(to_spectrum, ('row', 'col'), split_axis=0, concat_axis=3,...]
    convert_element_type x2 -> x0, local copies, waits for them, and re-layouts: 18.6 us -> none  [body(): to_spectrum = jnp.einsum('tlk,kcf->fctl', direction, dft_table, precision...]
    unnamed x34 -> x100, local copies, waits for them, and re-layouts: 112 us -> 103 us
where the time goes in v1:
time: 1090 us; the launch traced here: 1080 us
  matrix products  328 us (30%)
  blocking collectives  283 us (26%)
  local copies, waits for them, and re-layouts  203 us (19%)
  waiting for transfers between devices  155 us (14%)
  other arithmetic  93.1 us (9%)
  starting transfers between devices  11.5 us (1%)
    all_to_all x2, waiting for transfers between devices, to_taps(): lax.all_to_all(spectrum, ('row', 'col'), split_axis=3, concat_axis=0, til...  155 us
    all_to_all x2, blocking collectives, body(): lax.all_to_all(jnp.stack(jnp.split(to_spectrum, lax.axis_size(('row', 'co...  109 us
    unnamed x100, local copies, waits for them, and re-layouts  103 us
    all_to_all x1, blocking collectives, to_taps(): lax.all_to_all(spectrum, ('row', 'col'), split_axis=3, concat_axis=0, til...  98.5 us
    psum x2, blocking collectives, body(): lax.psum((along_term, jnp.sum(direction * image_taps)), ('row', 'col'))  75.5 us
    all_to_all x7, local copies, waits for them, and re-layouts, to_taps(): lax.all_to_all(spectrum, ('row', 'col'), split_axis=3, concat_axis=0, til...  58.6 us
    dot_general x3, matrix products, to_taps(): jnp.einsum('fctl,kcf->tlk', regrouped, dft_table, precision=lax.Precision...  57.9 us
    all_to_all x3, other arithmetic, to_taps(): lax.all_to_all(spectrum, ('row', 'col'), split_axis=3, concat_axis=0, til...  41.3 us
  transfers between devices with their start and end apart: 2, of which 2 were waited for; matrix products, arithmetic and copies ran while one was open for 3% of the time, Pallas kernels for 0%

profile of v1, /device:TPU:0, one launch (start us, length us, event | category | flops | bytes accessed | tf_op | source)
XLA Modules:
  0.0 1077.8 jit_solution(4105143637230933472)
XLA Ops:
  35.3 9.2 copy.57
  44.5 9.8 reshape.100
  54.3 8.0 all-to-all-start
  62.3 34.6 %sine_negate_fusion = (f32[1024,1,2048]{2,0,1:T(8,128)}, f32[1024,1,2048]{2,0,1:T(8,128)}) fusion(), kind=kLoop, calls=%fused_computation.57 | loop fusion | flops 31457280 | bytes 16777216 | tf_op jit(solution)/shard_map/neg | solution.py:16
  96.8 60.6 %all-to-all-done = f32[32,1,32768]{2,1,0:T(1,128)} async-done(((f32[32,1,32768]{2,1,0:T(1,128)}), f32[32,1,32768]{2,1,0:T(1,128)}, u32[]{:S(2)}, u32[]{:S(2)}) %all-to-all-start) | async-done | bytes 4194336 | tf_op jit(solution)/shard_map/all_to_all | solution.py:27
  158.0 13.8 %reduce = f32[32,32768]{1,0:T(8,128)} reduce(f32[32,1,32768]{2,1,0:T(1,128)} %all-to-all-done, f32[]{:T(128)} %broadcast.90), dimensions={1}, to_apply=%all_to_all.45.reduce_sub_computation | reduce | bytes 8388612 | tf_op jit(solution)/shard_map/all_to_all | solution.py:27
  171.7 7.4 reshape.101
  179.1 11.4 %copy.59 = f32[32,64,2,32,8]{1,0,4,2,3:T(8,128)} copy(f32[32,64,2,32,8]{1,3,2,4,0:T(8,128)} %bitcast.463) | data formatting | bytes 8388608 | tf_op jit(solution)/shard_map/all_to_all | solution.py:27
  190.5 7.8 all_to_all.48
  198.4 18.7 %fusion.81 = f32[32,8,1024]{2,1,0:T(8,128)S(1)} fusion(f32[2048,2,32,8]{0,3,1,2:T(8,128)} %all_to_all.48, f32[1024,1,2048]{2,0,1:T(8,128)} %get-tuple-element.20, f32[1024,1,2048]{2,0,1:T(8,128)} %get-tuple-element.21), kind=kOutput, calls=%fused_computation.92 | convolution fusion | flops 12893290496 | bytes 22020096 | tf_op jit(solution)/shard_map/fctl,kcf->tlk/dot_general | solution.py:30
  218.0 19.9 %fusion.66 = bf16[2048,2,32,8]{0,2,3,1:T(8,128)(2,1)S(1)} fusion(f32[32,8,1024]{2,1,0:T(8,128)S(1)} %fusion.81, f32[1024,1,2048]{2,0,1:T(8,128)} %get-tuple-element.20, f32[1024,1,2048]{2,0,1:T(8,128)} %get-tuple-element.21), kind=kOutput, calls=%fused_computation.75 | convolution fusion | flops 12894339072 | bytes 19922944 | tf_op jit(solution)/shard_map/tlk,kcf->fctl/dot_general | solution.py:55
  249.6 52.7 %all_to_all.64 = bf16[32,2,16384]{2,1,0:T(2,128)(2,1)} all-to-all(bf16[32,2,16384]{2,1,0:T(2,128)(2,1)S(1)} %reshape.102), channel_id=1, replica_groups=mesh['row'=4,'col'=8] {'row','col'}, dimensions={0} | all-to-all | bytes 4194304 | tf_op jit(solution)/shard_map/all_to_all | solution.py:59
  302.3 7.9 reshape.103
  319.9 12.7 %fusion.12 = f32[64,32,512]{2,1,0:T(8,128)} fusion(bf16[64,1,32,256]{3,2,0,1:T(8,128)(2,1)S(1)} %copy.83, bf16[64,2,512,256]{3,2,1,0:T(8,128)(2,1)} %param.6), kind=kOutput, calls=%fused_computation.13 | convolution fusion | flops 536870912 | bytes 22020096 | tf_op jit(solution)/shard_map/fml,ftl->ftm/dot_general | solution.py:78
  332.6 12.7 %fusion.34 = f32[64,32,512]{2,1,0:T(8,128)} fusion(bf16[64,1,32,256]{3,2,0,1:T(8,128)(2,1)S(1)} %copy.83, bf16[64,2,512,256]{3,2,1,0:T(8,128)(2,1)} %param.6), kind=kOutput, calls=%fused_computation.35 | convolution fusion | flops 536870912 | bytes 22020096 | tf_op jit(solution)/shard_map/fml,ftl->ftm/dot_general | solution.py:69
  348.4 12.7 %fusion.30 = f32[64,32,512]{2,1,0:T(8,128)} fusion(bf16[64,1,32,256]{3,2,0,1:T(8,128)(2,1)S(1)} %copy.84, bf16[64,2,512,256]{3,2,1,0:T(8,128)(2,1)} %param.6), kind=kOutput, calls=%fused_computation.31 | convolution fusion | flops 536870912 | bytes 22020096 | tf_op jit(solution)/shard_map/fml,ftl->ftm/dot_general | solution.py:75
  361.1 12.7 %fusion.14 = f32[64,32,512]{2,1,0:T(8,128)} fusion(bf16[64,1,32,256]{3,2,0,1:T(8,128)(2,1)S(1)} %copy.84, bf16[64,2,512,256]{3,2,1,0:T(8,128)(2,1)} %param.6), kind=kOutput, calls=%fused_computation.15 | convolution fusion | flops 536870912 | bytes 22020096 | tf_op jit(solution)/shard_map/fml,ftl->ftm/dot_general | solution.py:72
  373.8 11.9 %fusion.10 = f32[64,32,256]{2,1,0:T(8,128)} fusion(f32[64,32,512]{2,1,0:T(8,128)} %fusion.30, f32[64,32,512]{2,1,0:T(8,128)} %fusion.12, f32[32,512]{1,0:T(8,128)S(1)} %get-tuple-element.10, bf16[64,2,512,256]{3,2,1,0:T(8,128)(2,1)} %param.6), kind=kOutput, calls=%fused_computation.11 | convolution fusion | flops 540016640 | bytes 27328512 | tf_op jit(solution)/shard_map/fml,ftm->ftl/dot_general | solution.py:36
  385.8 11.9 %fusion.8 = f32[64,32,256]{2,1,0:T(8,128)} fusion(f32[64,32,512]{2,1,0:T(8,128)} %fusion.34, f32[64,32,512]{2,1,0:T(8,128)} %fusion.14, f32[32,512]{1,0:T(8,128)S(1)} %get-tuple-element.10, bf16[64,2,512,256]{3,2,1,0:T(8,128)(2,1)} %param.6), kind=kOutput, calls=%fused_computation.9 | convolution fusion | flops 540016640 | bytes 27328512 | tf_op jit(solution)/shard_map/fml,ftm->ftl/dot_general | solution.py:42
  397.7 12.8 %add_bitcast_fusion.3 = f32[64,1,32,256]{3,2,0,1:T(8,128)} fusion(f32[64,32,256]{2,1,0:T(8,128)} %fusion.10, f32[64,32,512]{2,1,0:T(8,128)} %fusion.34, f32[64,32,512]{2,1,0:T(8,128)} %fusion.14, f32[32,512]{1,0:T(8,128)S(1)} %get-tuple-element.10, bf16[64,1,32,256]{3,2,0,1:T(8,128)(2,1)S(1)} %copy.83, f32[64]{0:T(128)S(1)} %copy-done.11, ...), kind=kOutput, calls=%fused_computation.81 | convolution fusion | flops 542113792 | bytes 30474496 | tf_op jit(solution)/shard_map/fml,ftm->ftl/dot_general | solution.py:33
  410.5 13.1 %add_bitcast_fusion.2 = f32[64,1,32,256]{3,2,0,1:T(8,128)} fusion(f32[64,32,256]{2,1,0:T(8,128)} %fusion.8, f32[64,32,512]{2,1,0:T(8,128)} %fusion.30, f32[64,32,512]{2,1,0:T(8,128)} %fusion.12, f32[32,512]{1,0:T(8,128)S(1)} %get-tuple-element.10, bf16[64,1,32,256]{3,2,0,1:T(8,128)(2,1)S(1)} %copy.84, f32[64]{0:T(128)S(1)} %copy-done.11, ...), kind=kOutput, calls=%fused_computation.80 | convolution fusion | flops 542113792 | bytes 30474496 | tf_op jit(solution)/shard_map/fml,ftm->ftl/dot_general | solution.py:39
  427.5 9.2 copy.64
  436.7 9.8 reshape.104
  450.8 94.5 %all-to-all-done.2 = f32[32,1,32768]{2,1,0:T(1,128)} async-done(((f32[32,1,32768]{2,1,0:T(1,128)}), f32[32,1,32768]{2,1,0:T(1,128)}, u32[]{:S(2)}, u32[]{:S(2)}) %all-to-all-start.2) | async-done | bytes 4194336 | tf_op jit(solution)/shard_map/all_to_all | solution.py:27
  545.3 13.8 %reduce.1 = f32[32,32768]{1,0:T(8,128)} reduce(f32[32,1,32768]{2,1,0:T(1,128)} %all-to-all-done.2, f32[]{:T(128)} %broadcast.90), dimensions={1}, to_apply=%all_to_all.50.reduce_sub_computation | reduce | bytes 8388612 | tf_op jit(solution)/shard_map/all_to_all | solution.py:27
  566.4 11.4 %copy.66 = f32[32,64,2,32,8]{1,0,4,2,3:T(8,128)} copy(f32[32,64,2,32,8]{1,3,2,4,0:T(8,128)} %bitcast.464) | data formatting | bytes 8388608 | tf_op jit(solution)/shard_map/all_to_all | solution.py:27
  577.8 7.9 all_to_all.53
  585.8 19.5 %multiply_reduce_fusion.2 = (f32[]{:T(128)}, f32[]{:T(128)}, f32[32,8,1024]{2,1,0:T(8,128)S(1)}) fusion(f32[32,8,1024]{2,1,0:T(8,128)S(1)} %copy-done.5, f32[2048,2,32,8]{0,3,1,2:T(8,128)} %all_to_all.53, f32[1024,1,2048]{2,0,1:T(8,128)} %get-tuple-element.20, f32[1024,1,2048]{2,0,1:T(8,128)} %get-tuple-element.21), kind=kOutput, calls=%fused_computation.113 | convolution fusion | flops 12894339072 | bytes 23068680 | tf_op jit(solution)/shard_map/fctl,kcf->tlk/dot_general | solution.py:30
  605.3 37.4 %all-reduce.1 = (f32[]{:T(128)}, f32[]{:T(128)}) all-reduce(f32[]{:T(128)} %get-tuple-element.5, f32[]{:T(128)} %get-tuple-element.4), channel_id=1, replica_groups=mesh['row'=4,'col'=8] {'row','col'}, use_global_device_ids=true, to_apply=%region_1.2 | all-reduce | flops 2 | bytes 16 | tf_op jit(solution)/shard_map/psum | solution.py:94
  644.3 20.3 %fusion.63 = bf16[2048,2,32,8]{0,2,3,1:T(8,128)(2,1)S(1)} fusion(f32[32,8,1024]{2,1,0:T(8,128)S(1)} %multiply_add_fusion.1, f32[1024,1,2048]{2,0,1:T(8,128)} %get-tuple-element.20, f32[1024,1,2048]{2,0,1:T(8,128)} %get-tuple-element.21), kind=kOutput, calls=%fused_computation.74 | convolution fusion | flops 12894339072 | bytes 19922944 | tf_op jit(solution)/shard_map/tlk,kcf->fctl/dot_general | solution.py:55
  676.3 55.8 %all_to_all.65 = bf16[32,2,16384]{2,1,0:T(2,128)(2,1)} all-to-all(bf16[32,2,16384]{2,1,0:T(2,128)(2,1)S(1)} %reshape.106), channel_id=1, replica_groups=mesh['row'=4,'col'=8] {'row','col'}, dimensions={0} | all-to-all | bytes 4194304 | tf_op jit(solution)/shard_map/all_to_all | solution.py:59
  732.1 7.9 reshape.107
  749.7 12.7 %fusion.4 = f32[64,32,512]{2,1,0:T(8,128)} fusion(bf16[64,1,32,256]{3,2,0,1:T(8,128)(2,1)S(1)} %copy.85, bf16[64,2,512,256]{3,2,1,0:T(8,128)(2,1)} %param.6), kind=kOutput, calls=%fused_computation.5 | convolution fusion | flops 536870912 | bytes 22020096 | tf_op jit(solution)/shard_map/fml,ftl->ftm/dot_general | solution.py:78
  762.4 12.7 %fusion.26 = f32[64,32,512]{2,1,0:T(8,128)} fusion(bf16[64,1,32,256]{3,2,0,1:T(8,128)(2,1)S(1)} %copy.85, bf16[64,2,512,256]{3,2,1,0:T(8,128)(2,1)} %param.6), kind=kOutput, calls=%fused_computation.27 | convolution fusion | flops 536870912 | bytes 22020096 | tf_op jit(solution)/shard_map/fml,ftl->ftm/dot_general | solution.py:69
  778.0 12.7 %fusion.22 = f32[64,32,512]{2,1,0:T(8,128)} fusion(bf16[64,1,32,256]{3,2,0,1:T(8,128)(2,1)S(1)} %copy.86, bf16[64,2,512,256]{3,2,1,0:T(8,128)(2,1)} %param.6), kind=kOutput, calls=%fused_computation.23 | convolution fusion | flops 536870912 | bytes 22020096 | tf_op jit(solution)/shard_map/fml,ftl->ftm/dot_general | solution.py:75
  790.7 12.7 %fusion.6 = f32[64,32,512]{2,1,0:T(8,128)} fusion(bf16[64,1,32,256]{3,2,0,1:T(8,128)(2,1)S(1)} %copy.86, bf16[64,2,512,256]{3,2,1,0:T(8,128)(2,1)} %param.6), kind=kOutput, calls=%fused_computation.7 | convolution fusion | flops 536870912 | bytes 22020096 | tf_op jit(solution)/shard_map/fml,ftl->ftm/dot_general | solution.py:72
  803.4 11.9 %fusion.2 = f32[64,32,256]{2,1,0:T(8,128)} fusion(f32[64,32,512]{2,1,0:T(8,128)} %fusion.22, f32[64,32,512]{2,1,0:T(8,128)} %fusion.4, f32[32,512]{1,0:T(8,128)S(1)} %get-tuple-element.10, bf16[64,2,512,256]{3,2,1,0:T(8,128)(2,1)} %param.6), kind=kOutput, calls=%fused_computation.3 | convolution fusion | flops 540016640 | bytes 27328512 | tf_op jit(solution)/shard_map/fml,ftm->ftl/dot_general | solution.py:36
  815.3 11.9 %fusion = f32[64,32,256]{2,1,0:T(8,128)} fusion(f32[64,32,512]{2,1,0:T(8,128)} %fusion.26, f32[64,32,512]{2,1,0:T(8,128)} %fusion.6, f32[32,512]{1,0:T(8,128)S(1)} %get-tuple-element.10, bf16[64,2,512,256]{3,2,1,0:T(8,128)(2,1)} %param.6), kind=kOutput, calls=%fused_computation.1 | convolution fusion | flops 540016640 | bytes 27328512 | tf_op jit(solution)/shard_map/fml,ftm->ftl/dot_general | solution.py:42
  827.2 12.8 %add_bitcast_fusion.1 = f32[64,1,32,256]{3,2,0,1:T(8,128)} fusion(f32[64,32,256]{2,1,0:T(8,128)} %fusion.2, f32[64,32,512]{2,1,0:T(8,128)} %fusion.26, f32[64,32,512]{2,1,0:T(8,128)} %fusion.6, f32[32,512]{1,0:T(8,128)S(1)} %get-tuple-element.10, bf16[64,1,32,256]{3,2,0,1:T(8,128)(2,1)S(1)} %copy.85, f32[64]{0:T(128)S(1)} %copy-done.11, ...), kind=kOutput, calls=%fused_computation.79 | convolution fusion | flops 542113792 | bytes 30474496 | tf_op jit(solution)/shard_map/fml,ftm->ftl/dot_general | solution.py:33
  840.0 13.1 %add_bitcast_fusion = f32[64,1,32,256]{3,2,0,1:T(8,128)} fusion(f32[64,32,256]{2,1,0:T(8,128)} %fusion, f32[64,32,512]{2,1,0:T(8,128)} %fusion.22, f32[64,32,512]{2,1,0:T(8,128)} %fusion.4, f32[32,512]{1,0:T(8,128)S(1)} %get-tuple-element.10, bf16[64,1,32,256]{3,2,0,1:T(8,128)(2,1)S(1)} %copy.86, f32[64]{0:T(128)S(1)} %copy-done.11, ...), kind=kOutput, calls=%fused_computation.78 | convolution fusion | flops 542113792 | bytes 30474496 | tf_op jit(solution)/shard_map/fml,ftm->ftl/dot_general | solution.py:39
  857.1 9.2 copy.71
  866.3 9.8 reshape.108
  876.2 98.5 %all_to_all.66 = f32[32,1,32768]{2,1,0:T(1,128)} all-to-all(f32[32,1,32768]{2,1,0:T(1,128)} %reshape.108), channel_id=1, replica_groups=mesh['row'=4,'col'=8] {'row','col'}, dimensions={0} | all-to-all | bytes 8388608 | tf_op jit(solution)/shard_map/all_to_all | solution.py:27
  974.7 13.8 %reduce.2 = f32[32,32768]{1,0:T(8,128)} reduce(f32[32,1,32768]{2,1,0:T(1,128)} %all_to_all.66, f32[]{:T(128)} %broadcast.90), dimensions={1}, to_apply=%all_to_all.55.reduce_sub_computation | reduce | bytes 8388612 | tf_op jit(solution)/shard_map/all_to_all | solution.py:27
  995.8 11.4 %copy.73 = f32[32,64,2,32,8]{1,0,4,2,3:T(8,128)} copy(f32[32,64,2,32,8]{1,3,2,4,0:T(8,128)} %bitcast.465) | data formatting | bytes 8388608 | tf_op jit(solution)/shard_map/all_to_all | solution.py:27
  1007.3 8.0 all_to_all.58
  1015.3 19.6 %multiply_reduce_fusion = (f32[]{:T(128)}, f32[]{:T(128)}, f32[32,8,1024]{2,1,0:T(8,128)}) fusion(f32[32,8,1024]{2,1,0:T(8,128)S(1)} %copy-done.10, f32[32,8,1024]{2,1,0:T(8,128)S(1)} %copy-done.6, f32[32,8,1024]{2,1,0:T(8,128)S(1)} %copy-done.8, f32[]{:T(128)S(6)} %div.14, f32[2048,2,32,8]{0,3,1,2:T(8,128)} %all_to_all.58, ...), kind=kOutput, calls=%fused_computation.109 | convolution fusion | flops 12894863360 | bytes 25165836 | tf_op jit(solution)/shard_map/fctl,kcf->tlk/dot_general | solution.py:30
  1034.9 38.1 %all-reduce = (f32[]{:T(128)}, f32[]{:T(128)}) all-reduce(f32[]{:T(128)} %get-tuple-element.3, f32[]{:T(128)} %get-tuple-element.2), channel_id=1, replica_groups=mesh['row'=4,'col'=8] {'row','col'}, use_global_device_ids=true, to_apply=%region_5.6 | all-reduce | flops 2 | bytes 16 | tf_op jit(solution)/shard_map/psum | solution.py:94
  (115 shorter events, 114.2 us)
Async XLA Ops:
  54.3 103.1 %all-to-all-start = ((f32[32,1,32768]{2,1,0:T(1,128)}), f32[32,1,32768]{2,1,0:T(1,128)}, u32[]{:S(2)}, u32[]{:S(2)}) async-start(f32[32,1,32768]{2,1,0:T(1,128)} %reshape.100), calls=%async_computation | async-start | bytes 8388608 | tf_op jit(solution)/shard_map/all_to_all | solution.py:27
  217.1 1.0 copy-start.4
  240.8 1.9 copy-start.2
  385.8 11.9 %copy-start.11 = (f32[64]{0:T(128)S(1)}, f32[64]{0:T(128)}, u32[]{:S(2)}) copy-start(f32[64]{0:T(128)} %param.10) | copy-start | bytes 772
  410.5 13.1 %copy-start.1 = (f32[64,1,32,256]{3,2,0,1:T(8,128)S(1)}, f32[64,1,32,256]{3,2,0,1:T(8,128)}, u32[]{:S(2)}) copy-start(f32[64,1,32,256]{3,2,0,1:T(8,128)} %add_bitcast_fusion.3) | copy-start | bytes 6291460
  446.6 98.7 %all-to-all-start.2 = ((f32[32,1,32768]{2,1,0:T(1,128)}), f32[32,1,32768]{2,1,0:T(1,128)}, u32[]{:S(2)}, u32[]{:S(2)}) async-start(f32[32,1,32768]{2,1,0:T(1,128)} %reshape.104), calls=%async_computation.2 | async-start | bytes 8388608 | tf_op jit(solution)/shard_map/all_to_all | solution.py:27
  577.8 7.9 copy-start.5
  605.3 59.3 %copy-start.7 = (f32[32,8,1024]{2,1,0:T(8,128)}, f32[32,8,1024]{2,1,0:T(8,128)S(1)}, u32[]{:S(2)}) copy-start(f32[32,8,1024]{2,1,0:T(8,128)S(1)} %get-tuple-element.18) | copy-start | bytes 3145732
  644.3 20.3 %copy-start.9 = (f32[32,8,1024]{2,1,0:T(8,128)}, f32[32,8,1024]{2,1,0:T(8,128)S(1)}, u32[]{:S(2)}) copy-start(f32[32,8,1024]{2,1,0:T(8,128)S(1)} %multiply_add_fusion.1) | copy-start | bytes 3145732
  667.5 1.9 copy-start.3
  840.0 13.1 %copy-start = (f32[64,1,32,256]{3,2,0,1:T(8,128)S(1)}, f32[64,1,32,256]{3,2,0,1:T(8,128)}, u32[]{:S(2)}) copy-start(f32[64,1,32,256]{3,2,0,1:T(8,128)} %add_bitcast_fusion.1) | copy-start | bytes 6291460
  1007.3 8.0 copy-start.6
  1007.3 8.0 copy-start.8
  1007.3 8.0 copy-start.10
